TPU v7x, 32 devices: a whole 2x2x4 slice. The times are simulated.
32 devices in a mesh: dp: 8 (over z, y), mp: 4 (over x, core).
Axes of the slice: x: 2, y: 2, z: 4, core: 2. Of those that a mesh axis runs over, the one named last changes fastest.
Arguments:
- query_inputs: bfloat16 [128, 28672], P(None, 'mp'), may hold values from -0.09375 to 0.09375
- query_grads: bfloat16 [128, 8192], P(None, 'mp'), may hold values from -6 to 6
- basis_inputs: bfloat16 [28672, 28672], P('mp', 'dp'), may hold values from -0.03125 to 0.03125
- basis_grads: bfloat16 [8192, 8192], P('mp', 'dp'), may hold values from -0.0625 to 0.0625
- eig_inputs: float32 [28672], P('dp'), may hold values from 0.25 to 4
- eig_grads: float32 [8192], P('dp'), may hold values from 0.25 to 4
- train_inputs: bfloat16 [6144, 28672], P('dp', 'mp'), may hold values from -0.03540039 to 0.03540039
- train_grads: bfloat16 [6144, 8192], P('dp', 'mp'), may hold values from -0.06591797 to 0.06591797
Outputs:
- scores: float32 [4, 48], P('mp', 'dp')
All inputs are finite; a program needn't handle non-finite values.
Results may differ from a plain program's by a relative error of at most 0.0054.
Values may be sent and summed in bfloat16 or wider, within the bound.
A program may use at most 128 MiB of HBM per device.

v0:
```python
import jax
import jax.numpy as jnp
from jax import lax
from jax.sharding import PartitionSpec as P

LEN = 128
QLEN = 32


def per_device(
    query_inputs,
    query_grads,
    basis_inputs,
    basis_grads,
    eig_inputs,
    eig_grads,
    train_inputs,
    train_grads,
):
    input_cols = basis_inputs.shape[1]
    feat_in = basis_inputs.shape[0]
    row_count = query_inputs.shape[0] // lax.axis_size("mp")
    rot_in = jnp.dot(query_inputs, basis_inputs, preferred_element_type=jnp.float32)
    rot_out = jnp.dot(query_grads, basis_grads, preferred_element_type=jnp.float32)
    rotated = lax.psum_scatter(
        jnp.concatenate([rot_in, rot_out], axis=1), "mp", scatter_dimension=0, tiled=True
    )
    scaled = jnp.concatenate(
        [
            rotated[:, :input_cols] / eig_inputs[None, :],
            rotated[:, input_cols:] / eig_grads[None, :],
        ],
        axis=1,
    ).astype(jnp.bfloat16)
    segment = lax.all_gather(scaled, "mp", axis=0, tiled=True)
    back_in = jnp.einsum(
        "qc,fc->qf", segment[:, :input_cols], basis_inputs, preferred_element_type=jnp.float32
    )
    back_out = jnp.einsum(
        "qc,fc->qf", segment[:, input_cols:], basis_grads, preferred_element_type=jnp.float32
    )
    partial_value = jnp.concatenate([back_in, back_out], axis=1)
    shared_part = lax.psum_scatter(partial_value, "dp", scatter_dimension=0, tiled=True).astype(
        jnp.bfloat16
    )
    directions = lax.all_gather(shared_part, "dp", axis=0, tiled=True)
    train_count = train_inputs.shape[0]
    inner_in = jnp.einsum(
        "qf,tf->qt", directions[:, :feat_in], train_inputs, preferred_element_type=jnp.float32
    )
    inner_out = jnp.einsum(
        "qf,tf->qt", directions[:, feat_in:], train_grads, preferred_element_type=jnp.float32
    )
    pair_sums = lax.psum_scatter(
        jnp.concatenate([inner_in, inner_out], axis=1), "mp", scatter_dimension=0, tiled=True
    )
    products = pair_sums[:, :train_count] * pair_sums[:, train_count:]
    grouped = products.reshape(row_count // QLEN, QLEN, train_count // LEN, LEN)
    return jnp.sum(grouped, axis=(1, 3))


def solution(mesh):
    return jax.shard_map(
        per_device,
        mesh=mesh,
        in_specs=(
            P(None, "mp"),
            P(None, "mp"),
            P("mp", "dp"),
            P("mp", "dp"),
            P("dp"),
            P("dp"),
            P("dp", "mp"),
            P("dp", "mp"),
        ),
        out_specs=P("mp", "dp"),
        check_vma=False,
    )
```

profile of v0, /device:TPU:0, one launch (start us, length us, event | category | flops | bytes accessed | tf_op | source)
XLA Modules:
  0.0 314.6 jit_solution(5288105056165067332)
XLA Ops:
  6.5 0.0 copy-start
  6.5 0.0 reduce-scatter.4.cloned.1.call-start
  6.5 4.0 %fusion.12 = f32[128,1024]{1,0:T(8,128)} fusion(bf16[128,2048]{1,0:T(8,128)(2,1)} %param.9, bf16[2048,1024]{1,0:T(8,128)(2,1)} %param.11), kind=kOutput, calls=%fused_computation.20 | convolution fusion | flops 536870912 | bytes 5242880 | tf_op jit(solution)/shard_map/dot_general | solution.py:24
  10.6 20.9 %fusion.11 = f32[128,3584]{1,0:T(8,128)} fusion(bf16[128,7168]{1,0:T(8,128)(2,1)} %param.8, bf16[7168,3584]{1,0:T(8,128)(2,1)} %param.10), kind=kOutput, calls=%fused_computation.19 | convolution fusion | flops 6576668672 | bytes 55050240 | tf_op jit(solution)/shard_map/dot_general | solution.py:23
  31.5 0.0 copy-start.3
  31.5 0.0 copy-start.2
  31.5 3.3 %pad_maximum_fusion.1 = f32[128,4608]{1,0:T(8,128)} fusion(f32[128,1024]{1,0:T(8,128)} %fusion.12, f32[128,3584]{1,0:T(8,128)} %fusion.11), kind=kLoop, calls=%fused_computation.1 | loop fusion | flops 589824 | bytes 4718592 | tf_op jit(solution)/shard_map/concatenate | solution.py:26
  34.7 0.0 reduce-scatter.4.cloned.1.call-update
  34.8 0.0 all-gather.3.cloned.1.call-start
  34.8 35.6 %reduce-scatter.4.cloned.1.call-done = f32[32,4608]{1,0:T(8,128)} async-done(((f32[128,4608]{1,0:T(8,128)}), f32[32,4608]{1,0:T(8,128)}) %reduce-scatter.4.cloned.1.call-update) | async-done | bytes 589840 | tf_op jit(solution)/shard_map/reduce_scatter | solution.py:25
  70.4 0.0 copy-done.3
  70.5 0.9 fusion.9
  71.4 0.0 copy-done.2
  71.4 1.1 fusion.6
  72.4 0.7 pad_maximum_fusion.3
  73.2 0.0 all-gather.3.cloned.1.call-update
  73.2 0.0 reduce-scatter.6.cloned.1.call-start
  73.3 17.5 %all-gather.3.cloned.1.call-done = bf16[128,4608]{1,0:T(8,128)(2,1)} async-done(((bf16[32,4608]{1,0:T(8,128)(2,1)}), bf16[128,4608]{1,0:T(8,128)(2,1)}) %all-gather.3.cloned.1.call-update) | async-done | bytes 1179664 | tf_op jit(solution)/shard_map/all_gather | solution.py:35
  90.8 4.8 %fusion.7 = f32[128,2048]{1,0:T(8,128)} fusion(bf16[2048,1024]{1,0:T(8,128)(2,1)} %param.11, bf16[128,4608]{1,0:T(8,128)(2,1)} %all-gather.3.cloned.1.call-done), kind=kOutput, calls=%fused_computation.12 | convolution fusion | flops 536870912 | bytes 5505024 | tf_op jit(solution)/shard_map/qc,fc->qf/dot_general | solution.py:39
  95.6 23.4 %fusion.2 = f32[128,7168]{1,0:T(8,128)} fusion(bf16[7168,3584]{1,0:T(8,128)(2,1)} %param.10, bf16[128,4608]{1,0:T(8,128)(2,1)} %all-gather.3.cloned.1.call-done), kind=kOutput, calls=%fused_computation.4 | convolution fusion | flops 6576668672 | bytes 55967744 | tf_op jit(solution)/shard_map/qc,fc->qf/dot_general | solution.py:36
  119.0 4.9 %pad_maximum_fusion = f32[128,9216]{1,0:T(8,128)} fusion(f32[128,2048]{1,0:T(8,128)} %fusion.7, f32[128,7168]{1,0:T(8,128)} %fusion.2), kind=kLoop, calls=%fused_computation | loop fusion | flops 1179648 | bytes 9437184 | tf_op jit(solution)/shard_map/concatenate | solution.py:42
  123.9 0.0 reduce-scatter.6.cloned.1.call-update
  124.0 0.0 all-gather.5.cloned.1.call-start
  124.0 95.8 %reduce-scatter.6.cloned.1.call-done = f32[16,9216]{1,0:T(8,128)} async-done(((f32[128,9216]{1,0:T(8,128)}), f32[16,9216]{1,0:T(8,128)}) %reduce-scatter.6.cloned.1.call-update) | async-done | bytes 589840 | tf_op jit(solution)/shard_map/reduce_scatter | solution.py:43
  219.8 1.8 convert_element_type.4
  221.6 0.0 all-gather.5.cloned.1.call-update
  221.6 0.0 reduce-scatter.8.cloned.1.call-start
  221.7 51.6 %all-gather.5.cloned.1.call-done = bf16[128,9216]{1,0:T(8,128)(2,1)} async-done(((bf16[16,9216]{1,0:T(8,128)(2,1)}), bf16[128,9216]{1,0:T(8,128)(2,1)}) %all-gather.5.cloned.1.call-update) | async-done | bytes 2359312 | tf_op jit(solution)/shard_map/all_gather | solution.py:46
  273.3 0.0 copy-done
  273.3 0.0 copy-start.1
  273.3 2.4 fusion.4
  275.7 0.0 copy-done.1
  275.7 7.9 %fusion = f32[128,768]{1,0:T(8,128)S(1)} fusion(bf16[768,7168]{1,0:T(8,128)(2,1)} %param.14, bf16[128,9216]{1,0:T(8,128)(2,1)S(1)} %copy-done.1), kind=kOutput, calls=%fused_computation.2 | convolution fusion | flops 1409286144 | bytes 13238272 | tf_op jit(solution)/shard_map/qf,tf->qt/dot_general | solution.py:48
  283.6 1.0 pad_maximum_fusion.2
  284.5 0.0 reduce-scatter.8.cloned.1.call-update
  284.6 21.9 %reduce-scatter.8.cloned.1.call-done = f32[32,1536]{1,0:T(8,128)} async-done(((f32[128,1536]{1,0:T(8,128)}), f32[32,1536]{1,0:T(8,128)}) %reduce-scatter.8.cloned.1.call-update) | async-done | bytes 196624 | tf_op jit(solution)/shard_map/reduce_scatter | solution.py:54
  306.4 1.0 fusion.10
  307.4 0.6 bitcast_reduce_fusion
Async XLA Ops:
  6.5 266.8 %copy-start = (bf16[768,2048]{1,0:T(8,128)(2,1)S(1)}, bf16[768,2048]{1,0:T(8,128)(2,1)}, u32[]{:S(2)}) copy-start(bf16[768,2048]{1,0:T(8,128)(2,1)} %param.15) | copy-start | bytes 9437188
  6.5 63.9 %reduce-scatter.4.cloned.1.call-start = ((), (), s32[]{:S(2)}) async-start(), calls=%async_computation.3 | async-start | bytes 2949120 | tf_op jit(solution)/shard_map/reduce_scatter | solution.py:25
  31.5 39.0 %copy-start.3 = (f32[1024]{0:T(1024)S(1)}, f32[1024]{0:T(1024)}, u32[]{:S(2)}) copy-start(f32[1024]{0:T(1024)} %param.13) | copy-start | bytes 12292
  31.5 39.9 %copy-start.2 = (f32[3584]{0:T(1024)S(1)}, f32[3584]{0:T(1024)}, u32[]{:S(2)}) copy-start(f32[3584]{0:T(1024)} %param.12) | copy-start | bytes 43012
  34.8 56.0 %all-gather.3.cloned.1.call-start = ((), (), s32[]{:S(2)}) async-start(), calls=%async_computation.4 | async-start | bytes 1474560 | tf_op jit(solution)/shard_map/all_gather | solution.py:35
  73.2 146.6 %reduce-scatter.6.cloned.1.call-start = ((), (), s32[]{:S(2)}) async-start(), calls=%async_computation.5 | async-start | bytes 5308416 | tf_op jit(solution)/shard_map/reduce_scatter | solution.py:43
  124.0 149.3 %all-gather.5.cloned.1.call-start = ((), (), s32[]{:S(2)}) async-start(), calls=%async_computation.6 | async-start | bytes 2654208 | tf_op jit(solution)/shard_map/all_gather | solution.py:46
  221.6 84.8 %reduce-scatter.8.cloned.1.call-start = ((), (), s32[]{:S(2)}) async-start(), calls=%async_computation.7 | async-start | bytes 983040 | tf_op jit(solution)/shard_map/reduce_scatter | solution.py:54
  273.3 2.4 copy-start.1
Sparse Core Ops, SparseCore 0:
  34.9 35.5 reduce-scatter.3
  73.3 17.4 all-gather.2
  124.1 95.6 reduce-scatter.5
  221.8 51.4 all-gather.4
  284.7 21.7 reduce-scatter.7
where the time goes:
time: 315 us
  waiting for transfers between devices  223 us (71%)
  matrix products  63.3 us (20%)
  other arithmetic  15.3 us (5%)
  between operations  13.2 us (4%)
    reduce_scatter x1, waiting for transfers between devices, per_device(): lax.psum_scatter(partial_value, 'dp', scatter_dimension=0, tiled=True)  95.8 us
    all_gather x1, waiting for transfers between devices, per_device(): directions = lax.all_gather(shared_part, 'dp', axis=0, tiled=True)  51.6 us
    reduce_scatter x1, waiting for transfers between devices, per_device(): lax.psum_scatter(jnp.concatenate([rot_in, rot_out], axis=1), 'mp', scatte...  35.6 us
    dot_general x1, matrix products, per_device(): jnp.einsum('qc,fc->qf', segment[:, :input_cols], basis_inputs, preferred_...  23.4 us
    reduce_scatter x1, waiting for transfers between devices, per_device(): lax.psum_scatter(jnp.concatenate([inner_in, inner_out], axis=1), 'mp', sc...  21.9 us
    dot_general x1, matrix products, per_device(): jnp.dot(query_inputs, basis_inputs, preferred_element_type=jnp.float32)  20.9 us
    all_gather x1, waiting for transfers between devices, per_device(): segment = lax.all_gather(scaled, 'mp', axis=0, tiled=True)  17.5 us
    dot_general x1, matrix products, per_device(): jnp.einsum('qf,tf->qt', directions[:, :feat_in], train_inputs, preferred_...  7.86 us
  transfers between devices with their start and end apart: 5, of which 5 were waited for; matrix products, arithmetic and copies ran while one was open for 0% of the time, Pallas kernels for 0%

commit v1 on v0

--- a/solution.py
+++ b/solution.py
@@ -43,7 +43,12 @@
     shared_part = lax.psum_scatter(partial_value, "dp", scatter_dimension=0, tiled=True).astype(
         jnp.bfloat16
     )
-    directions = lax.all_gather(shared_part, "dp", axis=0, tiled=True)
+    ring = [shared_part]
+    for hop in range(7):
+        ring.append(lax.ppermute(ring[-1], "dp", [(dev, (dev + 1) % 8) for dev in range(8)]))
+    directions = jnp.roll(
+        jnp.concatenate(ring[::-1], axis=0), (lax.axis_index("dp") + 1) * ring[0].shape[0], axis=0
+    )
     train_count = train_inputs.shape[0]
     inner_in = jnp.einsum(
         "qf,tf->qt", directions[:, :feat_in], train_inputs, preferred_element_type=jnp.float32

time: 315 us -> 337 us (1.070)
  waiting for transfers between devices: 223 us -> 238 us
  local copies, waits for them, and re-layouts: 0.02 us -> 10.9 us
  other arithmetic: 15.3 us -> 11.6 us
    ppermute x0 -> x7, waiting for transfers between devices: none -> 68.3 us  [per_device(): lax.ppermute(ring[-1], 'dp', [(dev, (dev + 1) % 8) for dev in range(8)])]
    all_gather x1 -> x0, waiting for transfers between devices: 51.6 us -> none  [per_device(): directions = lax.all_gather(shared_part, 'dp', axis=0, tiled=True)]
    unnamed x8 -> x42, local copies, waits for them, and re-layouts: 0.02 us -> 10.9 us
  transfers between devices with their start and end apart: 5 -> 11, of which waited for: 5 -> 11; matrix products, arithmetic and copies ran while one was open for 0% -> 0% of each run, Pallas kernels for 0% -> 0%
where the time goes in v1:
time: 337 us; the launch traced here: 336 us
  waiting for transfers between devices  238 us (71%)
  matrix products  60.6 us (18%)
  between operations  13.4 us (4%)
  other arithmetic  11.6 us (3%)
  local copies, waits for them, and re-layouts  10.9 us (3%)
    reduce_scatter x1, waiting for transfers between devices, per_device(): lax.psum_scatter(partial_value, 'dp', scatter_dimension=0, tiled=True)  95.8 us
    ppermute x7, waiting for transfers between devices, per_device(): lax.ppermute(ring[-1], 'dp', [(dev, (dev + 1) % 8) for dev in range(8)])  68.3 us
    reduce_scatter x1, waiting for transfers between devices, per_device(): lax.psum_scatter(jnp.concatenate([rot_in, rot_out], axis=1), 'mp', scatte...  35.6 us
    dot_general x1, matrix products, per_device(): jnp.einsum('qc,fc->qf', segment[:, :input_cols], basis_inputs, preferred_...  23.3 us
    dot_general x1, matrix products, per_device(): jnp.dot(query_inputs, basis_inputs, preferred_element_type=jnp.float32)  21.1 us
    reduce_scatter x1, waiting for transfers between devices, per_device(): lax.psum_scatter(jnp.concatenate([inner_in, inner_out], axis=1), 'mp', sc...  20.6 us
    all_gather x1, waiting for transfers between devices, per_device(): segment = lax.all_gather(scaled, 'mp', axis=0, tiled=True)  17.5 us
    unnamed x42, local copies, waits for them, and re-layouts  10.9 us
  transfers between devices with their start and end apart: 11, of which 11 were waited for; matrix products, arithmetic and copies ran while one was open for 0% of the time, Pallas kernels for 0%

profile of v1, /device:TPU:0, one launch (start us, length us, event | category | flops | bytes accessed | tf_op | source)
XLA Modules:
  0.0 336.0 jit_solution(2107968502903033077)
XLA Ops:
  6.5 21.1 %fusion.12 = f32[128,3584]{1,0:T(8,128)} fusion(bf16[128,7168]{1,0:T(8,128)(2,1)} %param.8, bf16[7168,3584]{1,0:T(8,128)(2,1)} %param.10), kind=kOutput, calls=%fused_computation.36 | convolution fusion | flops 6576668672 | bytes 55050240 | tf_op jit(solution)/shard_map/dot_general | solution.py:23
  27.6 3.2 fusion.13
  30.8 0.0 copy-start.12
  30.9 1.6 pad_maximum_fusion.1
  32.5 0.0 reduce-scatter.4.cloned.1.call-update
  32.5 0.0 all-gather.2.cloned.1.call-start
  32.5 35.6 %reduce-scatter.4.cloned.1.call-done = f32[32,4608]{1,0:T(8,128)} async-done(((f32[128,4608]{1,0:T(8,128)}), f32[32,4608]{1,0:T(8,128)}) %reduce-scatter.4.cloned.1.call-update) | async-done | bytes 589840 | tf_op jit(solution)/shard_map/reduce_scatter | solution.py:25
  68.2 1.1 fusion.6
  69.2 0.9 fusion.9
  70.2 0.7 pad_maximum_fusion.3
  70.9 0.0 all-gather.2.cloned.1.call-update
  70.9 0.0 reduce-scatter.6.cloned.1.call-start
  71.0 17.5 %all-gather.2.cloned.1.call-done = bf16[128,4608]{1,0:T(8,128)(2,1)} async-done(((bf16[32,4608]{1,0:T(8,128)(2,1)}), bf16[128,4608]{1,0:T(8,128)(2,1)}) %all-gather.2.cloned.1.call-update) | async-done | bytes 1179664 | tf_op jit(solution)/shard_map/all_gather | solution.py:35
  88.5 23.3 %fusion.2 = f32[128,7168]{1,0:T(8,128)} fusion(bf16[7168,3584]{1,0:T(8,128)(2,1)} %param.10, bf16[128,4608]{1,0:T(8,128)(2,1)} %all-gather.2.cloned.1.call-done), kind=kOutput, calls=%fused_computation.4 | convolution fusion | flops 6576668672 | bytes 55967744 | tf_op jit(solution)/shard_map/qc,fc->qf/dot_general | solution.py:36
  111.8 3.9 %fusion.7 = f32[128,2048]{1,0:T(8,128)S(1)} fusion(bf16[2048,1024]{1,0:T(8,128)(2,1)} %param.11, bf16[128,4608]{1,0:T(8,128)(2,1)} %all-gather.2.cloned.1.call-done), kind=kOutput, calls=%fused_computation.12 | convolution fusion | flops 536870912 | bytes 5505024 | tf_op jit(solution)/shard_map/qc,fc->qf/dot_general | solution.py:39
  115.8 2.5 pad_maximum_fusion
  118.3 0.0 reduce-scatter.6.cloned.1.call-update
  118.3 0.0 reduce-scatter.8.cloned.1.call-start
  118.3 95.8 %reduce-scatter.6.cloned.1.call-done = f32[16,9216]{1,0:T(8,128)} async-done(((f32[128,9216]{1,0:T(8,128)}), f32[16,9216]{1,0:T(8,128)}) %reduce-scatter.6.cloned.1.call-update) | async-done | bytes 589840 | tf_op jit(solution)/shard_map/reduce_scatter | solution.py:43
  214.1 1.1 convert_element_type.4
  215.2 1.5 collective-permute-start
  216.7 9.7 %collective-permute-done = bf16[16,9216]{1,0:T(8,128)(2,1)S(1)} collective-permute-done((bf16[16,9216]{1,0:T(8,128)(2,1)S(1)}, bf16[16,9216]{1,0:T(8,128)(2,1)S(1)}, u32[]{:S(2)}, u32[]{:S(2)}) %collective-permute-start) | collective-permute-done | bytes 294944 | tf_op jit(solution)/shard_map/ppermute | solution.py:48
  226.4 10.3 %collective-permute-done.1 = bf16[16,9216]{1,0:T(8,128)(2,1)S(1)} collective-permute-done((bf16[16,9216]{1,0:T(8,128)(2,1)S(1)}, bf16[16,9216]{1,0:T(8,128)(2,1)S(1)}, u32[]{:S(2)}, u32[]{:S(2)}) %collective-permute-start.1) | collective-permute-done | bytes 294944 | tf_op jit(solution)/shard_map/ppermute | solution.py:48
  236.7 0.7 copy-done.4
  237.4 9.4 %collective-permute-done.2 = bf16[16,9216]{1,0:T(8,128)(2,1)S(1)} collective-permute-done((bf16[16,9216]{1,0:T(8,128)(2,1)S(1)}, bf16[16,9216]{1,0:T(8,128)(2,1)S(1)}, u32[]{:S(2)}, u32[]{:S(2)}) %collective-permute-start.2) | collective-permute-done | bytes 294944 | tf_op jit(solution)/shard_map/ppermute | solution.py:48
  246.9 0.7 copy-done.6
  247.6 9.4 %collective-permute-done.3 = bf16[16,9216]{1,0:T(8,128)(2,1)S(1)} collective-permute-done((bf16[16,9216]{1,0:T(8,128)(2,1)S(1)}, bf16[16,9216]{1,0:T(8,128)(2,1)S(1)}, u32[]{:S(2)}, u32[]{:S(2)}) %collective-permute-start.3) | collective-permute-done | bytes 294944 | tf_op jit(solution)/shard_map/ppermute | solution.py:48
  257.0 0.7 copy-done.8
  257.7 9.4 %collective-permute-done.4 = bf16[16,9216]{1,0:T(8,128)(2,1)S(1)} collective-permute-done((bf16[16,9216]{1,0:T(8,128)(2,1)S(1)}, bf16[16,9216]{1,0:T(8,128)(2,1)S(1)}, u32[]{:S(2)}, u32[]{:S(2)}) %collective-permute-start.4) | collective-permute-done | bytes 294944 | tf_op jit(solution)/shard_map/ppermute | solution.py:48
  267.2 0.7 copy-done.10
  267.9 10.4 %collective-permute-done.5 = bf16[16,9216]{1,0:T(8,128)(2,1)} collective-permute-done((bf16[16,9216]{1,0:T(8,128)(2,1)S(1)}, bf16[16,9216]{1,0:T(8,128)(2,1)}, u32[]{:S(2)}, u32[]{:S(2)}) %collective-permute-start.5) | collective-permute-done | bytes 294944 | tf_op jit(solution)/shard_map/ppermute | solution.py:48
  278.3 9.7 %collective-permute-done.6 = bf16[16,9216]{1,0:T(8,128)(2,1)} collective-permute-done((bf16[16,9216]{1,0:T(8,128)(2,1)}, bf16[16,9216]{1,0:T(8,128)(2,1)}, u32[]{:S(2)}, u32[]{:S(2)}) %collective-permute-start.6) | collective-permute-done | bytes 294944 | tf_op jit(solution)/shard_map/ppermute | solution.py:48
  288.0 1.0 constant_dynamic-update-slice_fusion.15
  289.0 1.0 constant_dynamic-update-slice_fusion.14
  290.0 1.0 constant_dynamic-update-slice_fusion.13
  291.0 1.0 constant_dynamic-update-slice_fusion.12
  291.9 1.0 constant_dynamic-update-slice_fusion.11
  292.9 1.0 constant_dynamic-update-slice_fusion.10
  293.9 1.1 constant_dynamic-update-slice_fusion.8
  295.0 1.0 constant_dynamic-update-slice_fusion.7
  296.0 1.0 constant_dynamic-update-slice_fusion.6
  297.2 7.9 %fusion = f32[128,768]{1,0:T(8,128)S(1)} fusion(bf16[768,7168]{1,0:T(8,128)(2,1)} %param.14, bf16[256,9216]{1,0:T(8,128)(2,1)S(1)} %constant_dynamic-update-slice_fusion, s32[]{:T(128)S(6)} %select_n.14), kind=kOutput, calls=%fused_computation.2 | convolution fusion | flops 1409286144 | bytes 13238276 | tf_op jit(solution)/shard_map/qf,tf->qt/dot_general | solution.py:53
  305.1 1.2 fusion.4
  306.3 1.0 pad_maximum_fusion.2
  307.3 0.0 reduce-scatter.8.cloned.1.call-update
  307.3 20.6 %reduce-scatter.8.cloned.1.call-done = f32[32,1536]{1,0:T(8,128)} async-done(((f32[128,1536]{1,0:T(8,128)}), f32[32,1536]{1,0:T(8,128)}) %reduce-scatter.8.cloned.1.call-update) | async-done | bytes 196624 | tf_op jit(solution)/shard_map/reduce_scatter | solution.py:59
  327.9 1.0 fusion.10
  328.9 0.6 bitcast_reduce_fusion
  (37 shorter events, 0.2 us)
Async XLA Ops:
  6.5 298.6 %copy-start = (bf16[768,2048]{1,0:T(8,128)(2,1)S(1)}, bf16[768,2048]{1,0:T(8,128)(2,1)}, u32[]{:S(2)}) copy-start(bf16[768,2048]{1,0:T(8,128)(2,1)} %param.15) | copy-start | bytes 9437188
  6.5 61.6 %reduce-scatter.4.cloned.1.call-start = ((), (), s32[]{:S(2)}) async-start(), calls=%async_computation.3 | async-start | bytes 2949120 | tf_op jit(solution)/shard_map/reduce_scatter | solution.py:25
  27.6 3.2 copy-start.2
  30.8 37.3 %copy-start.12 = (f32[3584]{0:T(1024)S(1)}, f32[3584]{0:T(1024)}, u32[]{:S(2)}) copy-start(f32[3584]{0:T(1024)} %param.12) | copy-start | bytes 43012
  30.9 38.4 %copy-start.13 = (f32[1024]{0:T(1024)S(1)}, f32[1024]{0:T(1024)}, u32[]{:S(2)}) copy-start(f32[1024]{0:T(1024)} %param.13) | copy-start | bytes 12292
  32.5 56.0 %all-gather.2.cloned.1.call-start = ((), (), s32[]{:S(2)}) async-start(), calls=%async_computation.4 | async-start | bytes 1474560 | tf_op jit(solution)/shard_map/all_gather | solution.py:35
  70.9 143.2 %reduce-scatter.6.cloned.1.call-start = ((), (), s32[]{:S(2)}) async-start(), calls=%async_computation.5 | async-start | bytes 5308416 | tf_op jit(solution)/shard_map/reduce_scatter | solution.py:43
  111.8 3.9 %copy-start.1 = (f32[128,7168]{1,0:T(8,128)S(1)}, f32[128,7168]{1,0:T(8,128)}, u32[]{:S(2)}) copy-start(f32[128,7168]{1,0:T(8,128)} %fusion.2) | copy-start | bytes 11010052
  118.3 209.6 %reduce-scatter.8.cloned.1.call-start = ((), (), s32[]{:S(2)}) async-start(), calls=%async_computation.6 | async-start | bytes 983040 | tf_op jit(solution)/shard_map/reduce_scatter | solution.py:59
  215.2 11.2 %collective-permute-start = (bf16[16,9216]{1,0:T(8,128)(2,1)S(1)}, bf16[16,9216]{1,0:T(8,128)(2,1)S(1)}, u32[]{:S(2)}, u32[]{:S(2)}) collective-permute-start(bf16[16,9216]{1,0:T(8,128)(2,1)S(1)} %convert_element_type.4), channel_id=1, source_target_pairs={{0,4},{4,8},{8,12},{12,16},{16,20},{20,24},{24,28},{28,0},{1,5},{5... | collective-permute-start | bytes 884744 | tf_op jit(solution)/shard_map/ppermute | solution.py:48
  226.4 10.3 %collective-permute-start.1 = (bf16[16,9216]{1,0:T(8,128)(2,1)S(1)}, bf16[16,9216]{1,0:T(8,128)(2,1)S(1)}, u32[]{:S(2)}, u32[]{:S(2)}) collective-permute-start(bf16[16,9216]{1,0:T(8,128)(2,1)S(1)} %collective-permute-done), channel_id=1, source_target_pairs={{0,4},{4,8},{8,12},{12,16},{16,20},{20,24},{24,28},{28,0},{1,5},{5... | collective-permute-start | bytes 884744 | tf_op jit(solution)/shard_map/ppermute | solution.py:48
  236.7 0.7 copy-start.4
  237.4 9.4 %collective-permute-start.2 = (bf16[16,9216]{1,0:T(8,128)(2,1)S(1)}, bf16[16,9216]{1,0:T(8,128)(2,1)S(1)}, u32[]{:S(2)}, u32[]{:S(2)}) collective-permute-start(bf16[16,9216]{1,0:T(8,128)(2,1)S(1)} %collective-permute-done.1), channel_id=1, source_target_pairs={{0,4},{4,8},{8,12},{12,16},{16,20},{20,24},{24,28},{28,0},{1,5},{5... | collective-permute-start | bytes 884744 | tf_op jit(solution)/shard_map/ppermute | solution.py:48
  246.9 0.7 copy-start.6
  247.6 9.4 %collective-permute-start.3 = (bf16[16,9216]{1,0:T(8,128)(2,1)S(1)}, bf16[16,9216]{1,0:T(8,128)(2,1)S(1)}, u32[]{:S(2)}, u32[]{:S(2)}) collective-permute-start(bf16[16,9216]{1,0:T(8,128)(2,1)S(1)} %collective-permute-done.2), channel_id=1, source_target_pairs={{0,4},{4,8},{8,12},{12,16},{16,20},{20,24},{24,28},{28,0},{1,5},{5... | collective-permute-start | bytes 884744 | tf_op jit(solution)/shard_map/ppermute | solution.py:48
  257.0 0.7 copy-start.8
  257.7 9.4 %collective-permute-start.4 = (bf16[16,9216]{1,0:T(8,128)(2,1)S(1)}, bf16[16,9216]{1,0:T(8,128)(2,1)S(1)}, u32[]{:S(2)}, u32[]{:S(2)}) collective-permute-start(bf16[16,9216]{1,0:T(8,128)(2,1)S(1)} %collective-permute-done.3), channel_id=1, source_target_pairs={{0,4},{4,8},{8,12},{12,16},{16,20},{20,24},{24,28},{28,0},{1,5},{5... | collective-permute-start | bytes 884744 | tf_op jit(solution)/shard_map/ppermute | solution.py:48
  267.2 0.7 copy-start.10
  267.9 10.4 %collective-permute-start.5 = (bf16[16,9216]{1,0:T(8,128)(2,1)S(1)}, bf16[16,9216]{1,0:T(8,128)(2,1)}, u32[]{:S(2)}, u32[]{:S(2)}) collective-permute-start(bf16[16,9216]{1,0:T(8,128)(2,1)S(1)} %collective-permute-done.4), channel_id=1, source_target_pairs={{0,4},{4,8},{8,12},{12,16},{16,20},{20,24},{24,28},{28,0},{1,5},{5... | collective-permute-start | bytes 884744 | tf_op jit(solution)/shard_map/ppermute | solution.py:48
  278.3 9.7 %collective-permute-start.6 = (bf16[16,9216]{1,0:T(8,128)(2,1)}, bf16[16,9216]{1,0:T(8,128)(2,1)}, u32[]{:S(2)}, u32[]{:S(2)}) collective-permute-start(bf16[16,9216]{1,0:T(8,128)(2,1)} %collective-permute-done.5), channel_id=1, source_target_pairs={{0,4},{4,8},{8,12},{12,16},{16,20},{20,24},{24,28},{28,0},{1,5},{5... | collective-permute-start | bytes 884744 | tf_op jit(solution)/shard_map/ppermute | solution.py:48
  278.3 18.7 %copy-start.11 = (bf16[16,9216]{1,0:T(8,128)(2,1)S(1)}, bf16[16,9216]{1,0:T(8,128)(2,1)}, u32[]{:S(2)}) copy-start(bf16[16,9216]{1,0:T(8,128)(2,1)} %copy-done.10) | copy-start | bytes 884740
  278.3 18.8 %copy-start.9 = (bf16[16,9216]{1,0:T(8,128)(2,1)S(1)}, bf16[16,9216]{1,0:T(8,128)(2,1)}, u32[]{:S(2)}) copy-start(bf16[16,9216]{1,0:T(8,128)(2,1)} %copy-done.8) | copy-start | bytes 884740
  278.3 18.8 %copy-start.7 = (bf16[16,9216]{1,0:T(8,128)(2,1)S(1)}, bf16[16,9216]{1,0:T(8,128)(2,1)}, u32[]{:S(2)}) copy-start(bf16[16,9216]{1,0:T(8,128)(2,1)} %copy-done.6) | copy-start | bytes 884740
  278.3 18.9 %copy-start.5 = (bf16[16,9216]{1,0:T(8,128)(2,1)S(1)}, bf16[16,9216]{1,0:T(8,128)(2,1)}, u32[]{:S(2)}) copy-start(bf16[16,9216]{1,0:T(8,128)(2,1)} %copy-done.4) | copy-start | bytes 884740
  278.3 18.9 %copy-start.3 = (f32[16,9216]{1,0:T(8,128)S(1)}, f32[16,9216]{1,0:T(8,128)}, u32[]{:S(2)}) copy-start(f32[16,9216]{1,0:T(8,128)} %reduce-scatter.6.cloned.1.call-done) | copy-start | bytes 1769476
Sparse Core Ops, SparseCore 0:
  32.6 35.5 reduce-scatter.3
  71.0 17.4 all-gather.1
  118.4 95.6 reduce-scatter.5
  307.4 20.4 reduce-scatter.7
